TPU v7x, 32 devices: a whole 2x2x4 slice. The times are simulated.
32 devices in a mesh: ctx: 8 (over z, x), tp: 4 (over y, core).
Axes of the slice: x: 2, y: 2, z: 4, core: 2. Of those that a mesh axis runs over, the one named last changes fastest.
Arguments:
- q_nope: bfloat16 [8, 128, 128], P('ctx', 'tp'), may hold values from -6 to 6
- q_rope: bfloat16 [8, 128, 64], P('ctx', 'tp'), may hold values from -256 to 256
- w_uk: bfloat16 [128, 128, 512], P('tp'), may hold values from -0.5 to 0.5
- w_uv: bfloat16 [128, 512, 128], P('tp'), may hold values from -3 to 3
- w_out: bfloat16 [16384, 7168], P('tp', 'ctx'), may hold values from -0.046875 to 0.046875
- prefix_cache: bfloat16 [32768, 576], P('ctx'), may hold values from -6 to 6
- block_table: int32 [512], P('ctx'), may hold values from 0 to 511, each once
- prefix_len: int32 [8], replicated, may hold values from 8192 to 32768
- suffix_cache: bfloat16 [8, 256, 576], P('ctx'), may hold values from -12 to 12
- suffix_len: int32 [8], P('ctx'), may hold values from 2 to 256
Outputs:
- layer_out: bfloat16 [8, 7168], P('tp', 'ctx')
Inputs may be any that keep to these rules, and one draw needn't show every extreme that they name: A permutation: slots b * 64 to b * 64 + 63 of prefix_cache hold prefix positions block_table[b] * 64 onwards.
All inputs are finite; a program needn't handle non-finite values.
Results may differ from a plain program's by a relative error of at most 0.0078.
Values may be sent and summed in bfloat16 or wider, within the bound.
A program may use at most 64 MiB of HBM per device.

v0:
```python
import jax
import jax.numpy as jnp
from jax import lax
from jax.sharding import PartitionSpec as P

LAT = 512
ROPE = 64
NOPE = 128
BLOCK = 64
masked_value = -1e30


def partial_stats(scores, visible, values, pattern):
    row_peak = jnp.max(jnp.where(visible, scores, masked_value), axis=2)
    weights = jnp.where(visible, jnp.exp(scores - row_peak[:, :, None]), 0.0).astype(jnp.bfloat16)
    row_mass = jnp.sum(weights, axis=2, dtype=jnp.float32)
    row_weighted = jnp.einsum(pattern, weights, values, preferred_element_type=jnp.float32)
    return (row_peak, row_mass, row_weighted)


def value_project(latent, value_weight):
    return jnp.einsum("rhc,hcv->rhv", latent, value_weight, precision=lax.Precision.HIGHEST)


def on_device(
    q_nope,
    q_rope,
    w_uk,
    w_uv,
    w_out,
    prefix_cache,
    block_table,
    prefix_len,
    suffix_cache,
    suffix_len,
):
    softmax_scale = (NOPE + ROPE) ** (-0.5)
    q_latent = jnp.einsum("rhn,hnc->rhc", q_nope, w_uk, preferred_element_type=jnp.float32).astype(
        jnp.bfloat16
    )
    own_queries = jnp.concatenate([q_latent, q_rope], axis=2)
    all_queries = lax.all_gather(own_queries, "ctx", axis=0, tiled=True)
    ctx_count = lax.axis_size("ctx")
    own_count = own_queries.shape[0]
    value_weight = w_uv.astype(jnp.float32)
    positions = (
        block_table[:, None] * BLOCK + jnp.arange(BLOCK, dtype=jnp.int32)[None, :]
    ).reshape(-1)
    visible = (positions[None, :] < prefix_len[:, None])[:, None, :]
    scores = (
        jnp.einsum("rhc,tc->rht", all_queries, prefix_cache, preferred_element_type=jnp.float32)
        * softmax_scale
    )
    row_peak, row_mass, row_weighted = partial_stats(
        scores, visible, prefix_cache[:, :LAT], "rht,tc->rhc"
    )
    suffix_scores = (
        jnp.einsum("rhc,rtc->rht", own_queries, suffix_cache, preferred_element_type=jnp.float32)
        * softmax_scale
    )
    suffix_slots = jnp.arange(suffix_cache.shape[1], dtype=jnp.int32)
    suffix_visible = (suffix_slots[None, :] < suffix_len[:, None])[:, None, :]
    tail_peak, tail_mass, tail_weighted = partial_stats(
        suffix_scores, suffix_visible, suffix_cache[:, :, :LAT], "rht,rtc->rhc"
    )

    def by_owner(values):
        return values.reshape((ctx_count, own_count) + values.shape[1:])

    got_peak, got_mass, got_weighted = (
        lax.all_to_all(by_owner(row_peak), "ctx", split_axis=0, concat_axis=0, tiled=True),
        lax.all_to_all(by_owner(row_mass), "ctx", split_axis=0, concat_axis=0, tiled=True),
        lax.all_to_all(by_owner(row_weighted), "ctx", split_axis=0, concat_axis=0, tiled=True),
    )
    highest = jnp.maximum(jnp.max(got_peak, axis=0), tail_peak)
    factors = jnp.exp(got_peak - highest[None])
    tail_factor = jnp.exp(tail_peak - highest)
    total_mass = jnp.sum(factors * got_mass, axis=0) + tail_factor * tail_mass
    total_weighted = (
        jnp.sum(factors[..., None] * got_weighted, axis=0) + tail_factor[:, :, None] * tail_weighted
    )
    head_values = value_project(total_weighted / total_mass[:, :, None], value_weight).astype(
        jnp.bfloat16
    )
    flat_values = head_values.reshape(own_count, -1)
    every_value = lax.all_gather(flat_values, "ctx", axis=0, tiled=True)
    return lax.psum_scatter(
        jnp.dot(every_value, w_out, preferred_element_type=jnp.float32),
        "tp",
        scatter_dimension=0,
        tiled=True,
    ).astype(jnp.bfloat16)


def solution(mesh):
    placed = (
        P("ctx", "tp", None),
        P("ctx", "tp", None),
        P("tp", None, None),
        P("tp", None, None),
        P("tp", "ctx"),
        P("ctx", None),
        P("ctx"),
        P(),
        P("ctx", None, None),
        P("ctx"),
    )
    return jax.shard_map(
        on_device, mesh=mesh, in_specs=placed, out_specs=P("tp", "ctx"), check_vma=False
    )
```

profile of v0, /device:TPU:0, one launch (start us, length us, event | category | flops | bytes accessed | tf_op | source)
XLA Modules:
  0.0 129.5 jit_solution(10840114998855403633)
XLA Ops:
  0.0 0.7 broadcast_multiply_fusion
  0.8 0.1 add.38
  0.9 3.0 %fusion.20 = bf16[32,1,512]{2,1,0:T(2,128)(2,1)S(1)} fusion(bf16[32,128,512]{2,1,0:T(8,128)(2,1)} %param.12, bf16[32,128,1]{1,0,2:T(8,128)(2,1)S(1)} %bitcast.55), kind=kOutput, calls=%fused_computation.32 | convolution fusion | flops 4194304 | bytes 4235264 | tf_op jit(solution)/shard_map/rhn,hnc->rhc/dot_general | solution.py:38
  3.9 32.7 %all_gather.6 = bf16[8,32,576]{2,1,0:T(8,128)(2,1)S(1)} all-gather(bf16[1,32,576]{2,1,0:T(8,128)(2,1)S(1)} %pad_maximum_fusion), channel_id=1, replica_groups=mesh['ctx'=8,'tp'=4] {'ctx'}, dimensions={0}, use_global_device_ids=true | all-gather | bytes 331776 | tf_op jit(solution)/shard_map/all_gather | solution.py:42
  36.6 0.1 broadcast_compare_fusion
  36.7 2.7 %select_reduce_fusion = (f32[8,32]{1,0:T(8,128)}, f32[8,32,4096]{2,1,0:T(8,128)S(1)}) fusion(pred[8,4096]{1,0:T(8,128)(4,1)S(1)} %broadcast_compare_fusion, bf16[8,32,576]{2,1,0:T(8,128)(2,1)S(1)} %all_gather.6, bf16[4096,576]{0,1:T(8,128)(2,1)S(1)} %copy-done.5), kind=kOutput, calls=%fused_computation.7 | convolution fusion | flops 1211105024 | bytes 9241600 | tf_op jit(solution)/shard_map/rhc,tc->rht/dot_general | solution.py:51
  39.4 1.9 %copy-done.1 = f32[8,32,4096]{2,1,0:T(8,128)} copy-done((f32[8,32,4096]{2,1,0:T(8,128)}, f32[8,32,4096]{2,1,0:T(8,128)S(1)}, u32[]{:S(2)}) %copy-start.1) | copy-done | bytes 4194328
  41.3 1.7 %convert_reduce_fusion = f32[8,32]{1,0:T(8,128)S(1)} fusion(f32[8,32,4096]{2,1,0:T(8,128)S(1)} %get-tuple-element.10, f32[8,32]{1,0:T(8,128)} %get-tuple-element.9, pred[8,4096]{1,0:T(8,128)(4,1)S(1)} %broadcast_compare_fusion), kind=kLoop, calls=%fused_computation.4 | loop fusion | flops 5242624 | bytes 4229120 | tf_op jit(solution)/shard_map/reduce_sum | solution.py:16
  43.0 11.8 %all_to_all.15 = f32[8,1,32]{2,1,0:T(1,128)S(1)} all-to-all(f32[8,1,32]{2,1,0:T(1,128)S(1)} %bitcast.60), channel_id=1, replica_groups=mesh['ctx'=8,'tp'=4] {'ctx'}, dimensions={0} | all-to-all | bytes 2048 | tf_op jit(solution)/shard_map/all_to_all | solution.py:72
  54.9 3.2 %all-to-all-start = ((f32[8,1,32]{2,1,0:T(1,128)}), f32[8,1,32]{2,1,0:T(1,128)S(1)}, u32[]{:S(2)}, u32[]{:S(2)}) async-start(f32[8,1,32]{2,1,0:T(1,128)} %bitcast.5), calls=%async_computation | async-start | bytes 8192 | tf_op jit(solution)/shard_map/all_to_all | solution.py:71
  58.1 5.6 %fusion.4 = f32[8,1,32,512]{3,2,1,0:T(8,128)} fusion(bf16[4096,576]{0,1:T(8,128)(2,1)} %param.15, f32[8,32,4096]{2,1,0:T(8,128)} %copy-done.1, f32[8,32]{1,0:T(8,128)} %get-tuple-element.9, pred[8,4096]{1,0:T(8,128)(4,1)S(1)} %broadcast_compare_fusion), kind=kOutput, calls=%fused_computation.8 | convolution fusion | flops 1076887552 | bytes 8949760 | tf_op jit(solution)/shard_map/rht,tc->rhc/dot_general | solution.py:17
  63.7 0.8 all-to-all-done
  64.5 5.1 %all-to-all-start.1 = ((f32[8,1,32,512]{3,2,1,0:T(8,128)}), f32[8,1,32,512]{3,2,1,0:T(8,128)S(1)}, u32[]{:S(2)}, u32[]{:S(2)}) async-start(f32[8,1,32,512]{3,2,1,0:T(8,128)} %fusion.4), calls=%async_computation.1 | async-start | bytes 1048576 | tf_op jit(solution)/shard_map/all_to_all | solution.py:73
  70.3 0.7 dynamic-slice
  71.7 0.3 select_reduce_fusion.1
  72.0 0.2 convert_reduce_fusion.1
  72.2 7.8 %all-to-all-done.1 = f32[8,1,32,512]{3,2,1,0:T(8,128)S(1)} async-done(((f32[8,1,32,512]{3,2,1,0:T(8,128)}), f32[8,1,32,512]{3,2,1,0:T(8,128)S(1)}, u32[]{:S(2)}, u32[]{:S(2)}) %all-to-all-start.1) | async-done | bytes 524320 | tf_op jit(solution)/shard_map/all_to_all | solution.py:73
  80.0 0.1 multiply_reduce_fusion
  80.1 0.2 fusion.9
  80.3 3.5 %fusion.16 = f32[32,1,128]{2,1,0:T(1,128)S(1)} fusion(bf16[32,512,128]{2,1,0:T(8,128)(2,1)} %param.13, f32[32,512,1]{1,0,2:T(8,128)S(1)} %fusion.9), kind=kOutput, calls=%fused_computation.22 | convolution fusion | flops 25165824 | bytes 4276224 | tf_op jit(solution)/shard_map/rhc,hcv->rhv/dot_general | solution.py:22
  83.9 30.5 %all-gather = bf16[8,1,4096]{2,1,0:T(2,128)(2,1)S(1)} all-gather(bf16[1,1,4096]{2,1,0:T(2,128)(2,1)S(1)} %reshape.166), channel_id=1, replica_groups=mesh['ctx'=8,'tp'=4] {'ctx'}, dimensions={0}, use_global_device_ids=true | all-gather | bytes 73728 | tf_op jit(solution)/shard_map/all_gather | solution.py:86
  114.4 4.1 %fusion.13 = f32[8,896]{1,0:T(8,128)S(1)} fusion(bf16[4096,896]{1,0:T(8,128)(2,1)} %param.14, bf16[8,1,4096]{2,1,0:T(2,128)(2,1)S(1)} %all-gather), kind=kOutput, calls=%fused_computation.18 | convolution fusion | flops 58720256 | bytes 7434240 | tf_op jit(solution)/shard_map/dot_general | solution.py:88
  118.6 10.3 %all-reduce = bf16[8,896]{1,0:T(8,128)(2,1)S(1)} all-reduce(f32[8,896]{1,0:T(8,128)S(1)} %fusion.13), channel_id=2, replica_groups=mesh['ctx'=8,'tp'=4] {'tp'}, use_global_device_ids=true, to_apply=%region_7.8.clone | all-reduce | flops 7168 | bytes 43008
  128.9 0.6 dynamic-slice_convert_fusion
  (23 shorter events, 0.2 us)
Async XLA Ops:
  0.0 0.9 copy-start
  0.0 3.9 %copy-start.3 = (bf16[1,32,64]{2,1,0:T(8,128)(2,1)S(1)}, bf16[1,32,64]{2,1,0:T(8,128)(2,1)}, u32[]{:S(2)}) copy-start(bf16[1,32,64]{2,1,0:T(8,128)(2,1)} %param.11) | copy-start | bytes 12292
  0.0 36.6 %copy-start.4 = (s32[8]{0:T(128)S(1)}, s32[8]{0:T(128)}, u32[]{:S(2)}) copy-start(s32[8]{0:T(128)} %param.17) | copy-start | bytes 100
  0.9 35.8 %copy-start.5 = (bf16[4096,576]{0,1:T(8,128)(2,1)S(1)}, bf16[4096,576]{0,1:T(8,128)(2,1)}, u32[]{:S(2)}) copy-start(bf16[4096,576]{0,1:T(8,128)(2,1)} %param.15) | copy-start | bytes 14155780
  39.4 1.9 %copy-start.1 = (f32[8,32,4096]{2,1,0:T(8,128)}, f32[8,32,4096]{2,1,0:T(8,128)S(1)}, u32[]{:S(2)}) copy-start(f32[8,32,4096]{2,1,0:T(8,128)S(1)} %get-tuple-element.10) | copy-start | bytes 12582916
  54.9 9.7 %all-to-all-start = ((f32[8,1,32]{2,1,0:T(1,128)}), f32[8,1,32]{2,1,0:T(1,128)S(1)}, u32[]{:S(2)}, u32[]{:S(2)}) async-start(f32[8,1,32]{2,1,0:T(1,128)} %bitcast.5), calls=%async_computation | async-start | bytes 8192 | tf_op jit(solution)/shard_map/all_to_all | solution.py:71
  58.1 12.2 %copy-start.6 = (u32[32]{0:T(128)S(1)}, u32[32]{0:T(128)}, u32[]{:S(2)}) copy-start(u32[32]{0:T(128)} %constant.17) | copy-start | bytes 388
  58.1 13.6 %copy-start.2 = (bf16[1,256,576]{1,2,0:T(8,128)(2,1)S(1)}, bf16[1,256,576]{1,2,0:T(8,128)(2,1)}, u32[]{:S(2)}) copy-start(bf16[1,256,576]{1,2,0:T(8,128)(2,1)} %param.18) | copy-start | bytes 884740
  64.5 15.5 %all-to-all-start.1 = ((f32[8,1,32,512]{3,2,1,0:T(8,128)}), f32[8,1,32,512]{3,2,1,0:T(8,128)S(1)}, u32[]{:S(2)}, u32[]{:S(2)}) async-start(f32[8,1,32,512]{3,2,1,0:T(8,128)} %fusion.4), calls=%async_computation.1 | async-start | bytes 1048576 | tf_op jit(solution)/shard_map/all_to_all | solution.py:73
where the time goes:
time: 130 us; the launch traced here: 129 us
  blocking collectives  85.4 us (66%)
  matrix products  19.4 us (15%)
  waiting for transfers between devices  8.58 us (7%)
  starting transfers between devices  8.34 us (6%)
  local copies, waits for them, and re-layouts  3.31 us (3%)
  other arithmetic  3 us (2%)
  between operations  1.49 us (1%)
    all_gather x1, blocking collectives, on_device(): all_queries = lax.all_gather(own_queries, 'ctx', axis=0, tiled=True)  32.7 us
    all_gather x1, blocking collectives, on_device(): every_value = lax.all_gather(flat_values, 'ctx', axis=0, tiled=True)  30.5 us
    all_to_all x1, blocking collectives, on_device(): lax.all_to_all(by_owner(row_mass), 'ctx', split_axis=0, concat_axis=0, ti...  11.8 us
    unnamed x1, blocking collectives  10.3 us
    all_to_all x1, waiting for transfers between devices, on_device(): lax.all_to_all(by_owner(row_weighted), 'ctx', split_axis=0, concat_axis=0...  7.78 us
    dot_general x2, matrix products, partial_stats(): jnp.einsum(pattern, weights, values, preferred_element_type=jnp.float32)  5.81 us
    all_to_all x1, starting transfers between devices, on_device(): lax.all_to_all(by_owner(row_weighted), 'ctx', split_axis=0, concat_axis=0...  5.12 us
    dot_general x1, matrix products, on_device(): jnp.dot(every_value, w_out, preferred_element_type=jnp.float32)  4.14 us
  transfers between devices with their start and end apart: 2, of which 2 were waited for; matrix products, arithmetic and copies ran while one was open for 5% of the time, Pallas kernels for 0%

commit v1 on v0

--- a/solution.py
+++ b/solution.py
@@ -8,6 +8,21 @@
 NOPE = 128
 BLOCK = 64
 masked_value = -1e30
+
+
+def work_around(x, axis, dim, make, out_dim):
+    ways, here, step = (lax.axis_size(axis), lax.axis_index(axis), x.shape[dim])
+    results = []
+    for far in range(ways):
+        arriving = (
+            lax.ppermute(x, axis, [(d, (d + 1) % ways) for d in range(ways)])
+            if far + 1 < ways
+            else x
+        )
+        results.append(make(x, (here - far) % ways * step))
+        x = arriving
+    line = jnp.concatenate(results[::-1], axis=out_dim)
+    return jnp.roll(line, (here + 1) * results[0].shape[out_dim], axis=out_dim)
 
 
 def partial_stats(scores, visible, values, pattern):
@@ -39,7 +54,6 @@
         jnp.bfloat16
     )
     own_queries = jnp.concatenate([q_latent, q_rope], axis=2)
-    all_queries = lax.all_gather(own_queries, "ctx", axis=0, tiled=True)
     ctx_count = lax.axis_size("ctx")
     own_count = own_queries.shape[0]
     value_weight = w_uv.astype(jnp.float32)
@@ -48,7 +62,15 @@
     ).reshape(-1)
     visible = (positions[None, :] < prefix_len[:, None])[:, None, :]
     scores = (
-        jnp.einsum("rhc,tc->rht", all_queries, prefix_cache, preferred_element_type=jnp.float32)
+        work_around(
+            own_queries,
+            "ctx",
+            0,
+            lambda shard, start: jnp.einsum(
+                "rhc,tc->rht", shard, prefix_cache, preferred_element_type=jnp.float32
+            ),
+            0,
+        )
         * softmax_scale
     )
     row_peak, row_mass, row_weighted = partial_stats(

time: 130 us -> 152 us (1.17)
  waiting for transfers between devices: 8.58 us -> 52.7 us
  blocking collectives: 85.4 us -> 49.7 us
  matrix products: 19.4 us -> 26.4 us
  other arithmetic: 3 us -> 6.28 us
  starting transfers between devices: 8.34 us -> 11.4 us
    ppermute x0 -> x7, waiting for transfers between devices: none -> 43.9 us  [work_around(): lax.ppermute(x, axis, [(d, (d + 1) % ways) for d in range(ways)])]
    all_gather x1 -> x0, blocking collectives: 32.7 us -> none  [on_device(): all_queries = lax.all_gather(own_queries, 'ctx', axis=0, tiled=True)]
    dot_general x1 -> x8, matrix products: 2.69 us -> 9.74 us  [on_device(): jnp.einsum('rhc,tc->rht', shard, prefix_cache, preferred_element_type=jnp...]
    all_to_all x1, blocking collectives: 11.8 us -> 8.85 us  [on_device(): lax.all_to_all(by_owner(row_mass), 'ctx', split_axis=0, concat_axis=0, ti...]
    ppermute x0 -> x7, starting transfers between devices: none -> 2.98 us  [work_around(): lax.ppermute(x, axis, [(d, (d + 1) % ways) for d in range(ways)])]
    reduce_max x0 -> x1, other arithmetic: none -> 1.84 us  [partial_stats(): row_peak = jnp.max(jnp.where(visible, scores, masked_value), axis=2)]
  transfers between devices with their start and end apart: 2 -> 9, of which waited for: 2 -> 9; matrix products, arithmetic and copies ran while one was open for 5% -> 6% of each run, Pallas kernels for 0% -> 0%
where the time goes in v1:
time: 152 us
  waiting for transfers between devices  52.7 us (35%)
  blocking collectives  49.7 us (33%)
  matrix products  26.4 us (17%)
  starting transfers between devices  11.4 us (8%)
  other arithmetic  6.28 us (4%)
  local copies, waits for them, and re-layouts  3.7 us (2%)
  between operations  1.53 us (1%)
    ppermute x7, waiting for transfers between devices, work_around(): lax.ppermute(x, axis, [(d, (d + 1) % ways) for d in range(ways)])  43.9 us
    all_gather x1, blocking collectives, on_device(): every_value = lax.all_gather(flat_values, 'ctx', axis=0, tiled=True)  30.6 us
    unnamed x1, blocking collectives  10.3 us
    dot_general x8, matrix products, on_device(): jnp.einsum('rhc,tc->rht', shard, prefix_cache, preferred_element_type=jnp...  9.74 us
    all_to_all x1, blocking collectives, on_device(): lax.all_to_all(by_owner(row_mass), 'ctx', split_axis=0, concat_axis=0, ti...  8.85 us
    all_to_all x1, waiting for transfers between devices, on_device(): lax.all_to_all(by_owner(row_weighted), 'ctx', split_axis=0, concat_axis=0...  8 us
    dot_general x2, matrix products, partial_stats(): jnp.einsum(pattern, weights, values, preferred_element_type=jnp.float32)  5.87 us
    all_to_all x1, starting transfers between devices, on_device(): lax.all_to_all(by_owner(row_weighted), 'ctx', split_axis=0, concat_axis=0...  5.17 us
  transfers between devices with their start and end apart: 9, of which 9 were waited for; matrix products, arithmetic and copies ran while one was open for 6% of the time, Pallas kernels for 0%

profile of v1, /device:TPU:0, one launch (start us, length us, event | category | flops | bytes accessed | tf_op | source)
XLA Modules:
  0.0 151.6 jit_solution(12705724135464203755)
XLA Ops:
  0.7 2.8 %fusion.27 = bf16[32,1,512]{2,1,0:T(2,128)(2,1)S(1)} fusion(bf16[32,128,512]{2,1,0:T(8,128)(2,1)} %param.12, bf16[32,128,1]{1,0,2:T(8,128)(2,1)S(1)} %bitcast.112), kind=kOutput, calls=%fused_computation.63 | convolution fusion | flops 4194304 | bytes 4235264 | tf_op jit(solution)/shard_map/rhn,hnc->rhc/dot_general | solution.py:53
  4.3 3.0 %collective-permute-start = (bf16[1,32,576]{2,1,0:T(8,128)(2,1)S(1)}, bf16[1,32,576]{2,1,0:T(8,128)(2,1)S(1)}, u32[]{:S(2)}, u32[]{:S(2)}) collective-permute-start(bf16[1,32,576]{2,1,0:T(8,128)(2,1)S(1)} %pad_maximum_fusion), channel_id=1, source_target_pairs={{0,4},{4,8},{8,12},{12,16},{16,20},{20,24},{24,28},{28,0},{1,5},{5... | collective-permute-start | bytes 110600 | tf_op jit(solution)/shard_map/ppermute | solution.py:18
  7.2 5.0 %collective-permute-done = bf16[1,32,576]{2,1,0:T(8,128)(2,1)S(1)} collective-permute-done((bf16[1,32,576]{2,1,0:T(8,128)(2,1)S(1)}, bf16[1,32,576]{2,1,0:T(8,128)(2,1)S(1)}, u32[]{:S(2)}, u32[]{:S(2)}) %collective-permute-start) | collective-permute-done | bytes 36896 | tf_op jit(solution)/shard_map/ppermute | solution.py:18
  12.2 6.7 %collective-permute-done.1 = bf16[1,32,576]{2,1,0:T(8,128)(2,1)S(1)} collective-permute-done((bf16[1,32,576]{2,1,0:T(8,128)(2,1)S(1)}, bf16[1,32,576]{2,1,0:T(8,128)(2,1)S(1)}, u32[]{:S(2)}, u32[]{:S(2)}) %collective-permute-start.1) | collective-permute-done | bytes 36896 | tf_op jit(solution)/shard_map/ppermute | solution.py:18
  18.9 6.7 %collective-permute-done.2 = bf16[1,32,576]{2,1,0:T(8,128)(2,1)S(1)} collective-permute-done((bf16[1,32,576]{2,1,0:T(8,128)(2,1)S(1)}, bf16[1,32,576]{2,1,0:T(8,128)(2,1)S(1)}, u32[]{:S(2)}, u32[]{:S(2)}) %collective-permute-start.2) | collective-permute-done | bytes 36896 | tf_op jit(solution)/shard_map/ppermute | solution.py:18
  25.6 6.7 %collective-permute-done.3 = bf16[1,32,576]{2,1,0:T(8,128)(2,1)S(1)} collective-permute-done((bf16[1,32,576]{2,1,0:T(8,128)(2,1)S(1)}, bf16[1,32,576]{2,1,0:T(8,128)(2,1)S(1)}, u32[]{:S(2)}, u32[]{:S(2)}) %collective-permute-start.3) | collective-permute-done | bytes 36896 | tf_op jit(solution)/shard_map/ppermute | solution.py:18
  33.0 6.4 %collective-permute-done.4 = bf16[1,32,576]{2,1,0:T(8,128)(2,1)S(1)} collective-permute-done((bf16[1,32,576]{2,1,0:T(8,128)(2,1)S(1)}, bf16[1,32,576]{2,1,0:T(8,128)(2,1)S(1)}, u32[]{:S(2)}, u32[]{:S(2)}) %collective-permute-start.4) | collective-permute-done | bytes 36896 | tf_op jit(solution)/shard_map/ppermute | solution.py:18
  39.5 6.5 %collective-permute-done.5 = bf16[1,32,576]{2,1,0:T(8,128)(2,1)S(1)} collective-permute-done((bf16[1,32,576]{2,1,0:T(8,128)(2,1)S(1)}, bf16[1,32,576]{2,1,0:T(8,128)(2,1)S(1)}, u32[]{:S(2)}, u32[]{:S(2)}) %collective-permute-start.5) | collective-permute-done | bytes 36896 | tf_op jit(solution)/shard_map/ppermute | solution.py:18
  46.9 5.9 %collective-permute-done.6 = bf16[1,32,576]{2,1,0:T(8,128)(2,1)S(1)} collective-permute-done((bf16[1,32,576]{2,1,0:T(8,128)(2,1)S(1)}, bf16[1,32,576]{2,1,0:T(8,128)(2,1)S(1)}, u32[]{:S(2)}, u32[]{:S(2)}) %collective-permute-start.6) | collective-permute-done | bytes 36896 | tf_op jit(solution)/shard_map/ppermute | solution.py:18
  52.8 3.2 %constant_dynamic-update-slice_fusion.15 = (f32[16,32,4096]{2,1,0:T(8,128)S(1)}, f32[1,32,4096]{2,1,0:T(8,128)S(1)}) fusion(bf16[4096,576]{0,1:T(8,128)(2,1)} %param.15, bf16[1,32,576]{2,1,0:T(8,128)(2,1)S(1)} %collective-permute-done.6), kind=kOutput, calls=%fused_computation.57 | convolution fusion | flops 150994944 | bytes 5804032 | tf_op jit(solution)/shard_map/rhc,tc->rht/dot_general | solution.py:69
  57.0 0.9 constant_dynamic-update-slice_fusion.13
  60.7 0.9 constant_dynamic-update-slice_fusion.9
  63.0 1.8 %select_reduce_fusion = f32[8,32]{1,0:T(8,128)} fusion(f32[16,32,4096]{2,1,0:T(8,128)S(1)} %constant_dynamic-update-slice_fusion, s32[]{:T(128)S(6)} %select_n.30, pred[8,4096]{1,0:T(8,128)(4,1)S(1)} %broadcast_compare_fusion), kind=kLoop, calls=%fused_computation.13 | loop fusion | flops 3145472 | bytes 4228100 | tf_op jit(solution)/shard_map/reduce_max | solution.py:29
  64.8 1.4 copy-done.2
  66.2 1.9 %convert_reduce_fusion = f32[8,32]{1,0:T(8,128)S(1)} fusion(f32[8,32]{1,0:T(8,128)} %select_reduce_fusion, f32[16,32,4096]{2,1,0:T(8,128)S(1)} %constant_dynamic-update-slice_fusion, s32[]{:T(128)S(6)} %select_n.30, pred[8,4096]{1,0:T(8,128)(4,1)S(1)} %broadcast_compare_fusion), kind=kLoop, calls=%fused_computation.10 | loop fusion | flops 6291200 | bytes 4229124 | tf_op jit(solution)/shard_map/reduce_sum | solution.py:31
  68.0 8.8 %all_to_all.15 = f32[8,1,32]{2,1,0:T(1,128)S(1)} all-to-all(f32[8,1,32]{2,1,0:T(1,128)S(1)} %bitcast.118), channel_id=1, replica_groups=mesh['ctx'=8,'tp'=4] {'ctx'}, dimensions={0} | all-to-all | bytes 2048 | tf_op jit(solution)/shard_map/all_to_all | solution.py:94
  76.9 3.2 %all-to-all-start = ((f32[8,1,32]{2,1,0:T(1,128)}), f32[8,1,32]{2,1,0:T(1,128)S(1)}, u32[]{:S(2)}, u32[]{:S(2)}) async-start(f32[8,1,32]{2,1,0:T(1,128)} %bitcast.20), calls=%async_computation | async-start | bytes 8192 | tf_op jit(solution)/shard_map/all_to_all | solution.py:93
  80.1 5.7 %fusion.3 = f32[8,1,32,512]{3,2,1,0:T(8,128)} fusion(bf16[4096,576]{0,1:T(8,128)(2,1)} %param.15, f32[16,32,4096]{2,1,0:T(8,128)} %copy-done.2, s32[]{:T(128)S(6)} %select_n.30, f32[8,32]{1,0:T(8,128)} %select_reduce_fusion, pred[8,4096]{1,0:T(8,128)(4,1)S(1)} %broadcast_compare_fusion), kind=kOutput, calls=%fused_computation.15 | convolution fusion | flops 1077936128 | bytes 8949764 | tf_op jit(solution)/shard_map/rht,tc->rhc/dot_general | solution.py:32
  86.6 5.2 %all-to-all-start.1 = ((f32[8,1,32,512]{3,2,1,0:T(8,128)}), f32[8,1,32,512]{3,2,1,0:T(8,128)S(1)}, u32[]{:S(2)}, u32[]{:S(2)}) async-start(f32[8,1,32,512]{3,2,1,0:T(8,128)} %fusion.3), calls=%async_computation.1 | async-start | bytes 1048576 | tf_op jit(solution)/shard_map/all_to_all | solution.py:95
  94.2 8.0 %all-to-all-done.1 = f32[8,1,32,512]{3,2,1,0:T(8,128)S(1)} async-done(((f32[8,1,32,512]{3,2,1,0:T(8,128)}), f32[8,1,32,512]{3,2,1,0:T(8,128)S(1)}, u32[]{:S(2)}, u32[]{:S(2)}) %all-to-all-start.1) | async-done | bytes 524320 | tf_op jit(solution)/shard_map/all_to_all | solution.py:95
  102.5 3.5 %fusion.15 = f32[32,1,128]{2,1,0:T(1,128)S(1)} fusion(bf16[32,512,128]{2,1,0:T(8,128)(2,1)} %param.13, f32[32,512,1]{1,0,2:T(8,128)S(1)} %fusion.8), kind=kOutput, calls=%fused_computation.29 | convolution fusion | flops 25165824 | bytes 4276224 | tf_op jit(solution)/shard_map/rhc,hcv->rhv/dot_general | solution.py:37
  106.0 30.6 %all-gather = bf16[8,1,4096]{2,1,0:T(2,128)(2,1)S(1)} all-gather(bf16[1,1,4096]{2,1,0:T(2,128)(2,1)S(1)} %reshape.203), channel_id=1, replica_groups=mesh['ctx'=8,'tp'=4] {'ctx'}, dimensions={0}, use_global_device_ids=true | all-gather | bytes 73728 | tf_op jit(solution)/shard_map/all_gather | solution.py:108
  136.6 4.1 %fusion.12 = f32[8,896]{1,0:T(8,128)S(1)} fusion(bf16[4096,896]{1,0:T(8,128)(2,1)} %param.14, bf16[8,1,4096]{2,1,0:T(2,128)(2,1)S(1)} %all-gather), kind=kOutput, calls=%fused_computation.25 | convolution fusion | flops 58720256 | bytes 7434240 | tf_op jit(solution)/shard_map/dot_general | solution.py:110
  140.7 10.3 %all-reduce = bf16[8,896]{1,0:T(8,128)(2,1)S(1)} all-reduce(f32[8,896]{1,0:T(8,128)S(1)} %fusion.12), channel_id=2, replica_groups=mesh['ctx'=8,'tp'=4] {'tp'}, use_global_device_ids=true, to_apply=%region_7.8.clone | all-reduce | flops 7168 | bytes 43008
  (50 shorter events, 10.7 us)
Async XLA Ops:
  0.0 0.7 copy-start
  4.3 8.0 %collective-permute-start = (bf16[1,32,576]{2,1,0:T(8,128)(2,1)S(1)}, bf16[1,32,576]{2,1,0:T(8,128)(2,1)S(1)}, u32[]{:S(2)}, u32[]{:S(2)}) collective-permute-start(bf16[1,32,576]{2,1,0:T(8,128)(2,1)S(1)} %pad_maximum_fusion), channel_id=1, source_target_pairs={{0,4},{4,8},{8,12},{12,16},{16,20},{20,24},{24,28},{28,0},{1,5},{5... | collective-permute-start | bytes 110600 | tf_op jit(solution)/shard_map/ppermute | solution.py:18
  12.2 6.7 %collective-permute-start.1 = (bf16[1,32,576]{2,1,0:T(8,128)(2,1)S(1)}, bf16[1,32,576]{2,1,0:T(8,128)(2,1)S(1)}, u32[]{:S(2)}, u32[]{:S(2)}) collective-permute-start(bf16[1,32,576]{2,1,0:T(8,128)(2,1)S(1)} %collective-permute-done), channel_id=1, source_target_pairs={{0,4},{4,8},{8,12},{12,16},{16,20},{20,24},{24,28},{28,0},{1,5},{5... | collective-permute-start | bytes 110600 | tf_op jit(solution)/shard_map/ppermute | solution.py:18
  18.9 6.7 %collective-permute-start.2 = (bf16[1,32,576]{2,1,0:T(8,128)(2,1)S(1)}, bf16[1,32,576]{2,1,0:T(8,128)(2,1)S(1)}, u32[]{:S(2)}, u32[]{:S(2)}) collective-permute-start(bf16[1,32,576]{2,1,0:T(8,128)(2,1)S(1)} %collective-permute-done.1), channel_id=1, source_target_pairs={{0,4},{4,8},{8,12},{12,16},{16,20},{20,24},{24,28},{28,0},{1,5},{5... | collective-permute-start | bytes 110600 | tf_op jit(solution)/shard_map/ppermute | solution.py:18
  25.6 6.7 %collective-permute-start.3 = (bf16[1,32,576]{2,1,0:T(8,128)(2,1)S(1)}, bf16[1,32,576]{2,1,0:T(8,128)(2,1)S(1)}, u32[]{:S(2)}, u32[]{:S(2)}) collective-permute-start(bf16[1,32,576]{2,1,0:T(8,128)(2,1)S(1)} %collective-permute-done.2), channel_id=1, source_target_pairs={{0,4},{4,8},{8,12},{12,16},{16,20},{20,24},{24,28},{28,0},{1,5},{5... | collective-permute-start | bytes 110600 | tf_op jit(solution)/shard_map/ppermute | solution.py:18
  32.3 7.0 %collective-permute-start.4 = (bf16[1,32,576]{2,1,0:T(8,128)(2,1)S(1)}, bf16[1,32,576]{2,1,0:T(8,128)(2,1)S(1)}, u32[]{:S(2)}, u32[]{:S(2)}) collective-permute-start(bf16[1,32,576]{2,1,0:T(8,128)(2,1)S(1)} %collective-permute-done.3), channel_id=1, source_target_pairs={{0,4},{4,8},{8,12},{12,16},{16,20},{20,24},{24,28},{28,0},{1,5},{5... | collective-permute-start | bytes 110600 | tf_op jit(solution)/shard_map/ppermute | solution.py:18
  39.4 6.7 %collective-permute-start.5 = (bf16[1,32,576]{2,1,0:T(8,128)(2,1)S(1)}, bf16[1,32,576]{2,1,0:T(8,128)(2,1)S(1)}, u32[]{:S(2)}, u32[]{:S(2)}) collective-permute-start(bf16[1,32,576]{2,1,0:T(8,128)(2,1)S(1)} %collective-permute-done.4), channel_id=1, source_target_pairs={{0,4},{4,8},{8,12},{12,16},{16,20},{20,24},{24,28},{28,0},{1,5},{5... | collective-permute-start | bytes 110600 | tf_op jit(solution)/shard_map/ppermute | solution.py:18
  46.1 6.7 %collective-permute-start.6 = (bf16[1,32,576]{2,1,0:T(8,128)(2,1)S(1)}, bf16[1,32,576]{2,1,0:T(8,128)(2,1)S(1)}, u32[]{:S(2)}, u32[]{:S(2)}) collective-permute-start(bf16[1,32,576]{2,1,0:T(8,128)(2,1)S(1)} %collective-permute-done.5), channel_id=1, source_target_pairs={{0,4},{4,8},{8,12},{12,16},{16,20},{20,24},{24,28},{28,0},{1,5},{5... | collective-permute-start | bytes 110600 | tf_op jit(solution)/shard_map/ppermute | solution.py:18
  46.9 9.2 %copy-start.1 = (bf16[4096,576]{0,1:T(8,128)(2,1)S(1)}, bf16[4096,576]{0,1:T(8,128)(2,1)}, u32[]{:S(2)}) copy-start(bf16[4096,576]{0,1:T(8,128)(2,1)} %param.15) | copy-start | bytes 14155780
  59.8 1.9 %copy-start.4 = (bf16[1,32,64]{2,1,0:T(8,128)(2,1)S(1)}, bf16[1,32,64]{2,1,0:T(8,128)(2,1)}, u32[]{:S(2)}) copy-start(bf16[1,32,64]{2,1,0:T(8,128)(2,1)} %param.11) | copy-start | bytes 12292
  62.9 3.2 %copy-start.2 = (f32[16,32,4096]{2,1,0:T(8,128)}, f32[16,32,4096]{2,1,0:T(8,128)S(1)}, u32[]{:S(2)}) copy-start(f32[16,32,4096]{2,1,0:T(8,128)S(1)} %constant_dynamic-update-slice_fusion) | copy-start | bytes 25165828
  76.9 9.7 %all-to-all-start = ((f32[8,1,32]{2,1,0:T(1,128)}), f32[8,1,32]{2,1,0:T(1,128)S(1)}, u32[]{:S(2)}, u32[]{:S(2)}) async-start(f32[8,1,32]{2,1,0:T(1,128)} %bitcast.20), calls=%async_computation | async-start | bytes 8192 | tf_op jit(solution)/shard_map/all_to_all | solution.py:93
  80.1 12.3 %copy-start.5 = (u32[32]{0:T(128)S(1)}, u32[32]{0:T(128)}, u32[]{:S(2)}) copy-start(u32[32]{0:T(128)} %constant.47) | copy-start | bytes 388
  80.1 13.5 %copy-start.3 = (bf16[1,256,576]{1,2,0:T(8,128)(2,1)S(1)}, bf16[1,256,576]{1,2,0:T(8,128)(2,1)}, u32[]{:S(2)}) copy-start(bf16[1,256,576]{1,2,0:T(8,128)(2,1)} %param.18) | copy-start | bytes 884740
  86.6 15.6 %all-to-all-start.1 = ((f32[8,1,32,512]{3,2,1,0:T(8,128)}), f32[8,1,32,512]{3,2,1,0:T(8,128)S(1)}, u32[]{:S(2)}, u32[]{:S(2)}) async-start(f32[8,1,32,512]{3,2,1,0:T(8,128)} %fusion.3), calls=%async_computation.1 | async-start | bytes 1048576 | tf_op jit(solution)/shard_map/all_to_all | solution.py:95
